TPU v7x, 32 devices: a whole 2x2x4 slice. The times are simulated.
32 devices in a mesh: grp: 4 (over z), fsdp: 8 (over y, x, core).
Axes of the slice: x: 2, y: 2, z: 4, core: 2. Of those that a mesh axis runs over, the one named last changes fastest.
Arguments:
- acts: bfloat16 [64, 128, 4096], P(('grp', 'fsdp'))
- out_grads: bfloat16 [64, 128, 1024], P(('grp', 'fsdp'))
- doc_lengths: int32 [64], P(('grp', 'fsdp')), may hold values from 32 to 128
- proj_in: bfloat16 [64, 4096], replicated, may hold values from -0.09375 to 0.09375
- proj_out: bfloat16 [64, 1024], replicated, may hold values from -0.1875 to 0.1875
- store_grads: bfloat16 [7168, 4096], P(('grp', 'fsdp')), may hold values from -6 to 6
- queries: bfloat16 [512, 4096], P('fsdp'), may hold values from -6 to 6
Outputs:
- new_grads: bfloat16 [64, 4096], P(('grp', 'fsdp'))
- store_scores: bfloat16 [7168, 512], P(('grp', 'fsdp'))
- new_scores: bfloat16 [64, 512], P(('grp', 'fsdp'))
All inputs are finite; a program needn't handle non-finite values.
Results may differ from a plain program's by a relative error of at most 0.012.
The roundings to bfloat16 on the way count: a program that leaves them out, or rounds other values in their place, can miss the bound.
Values may be sent and summed in bfloat16 or wider, within the bound.
A program may use at most 64 MiB of HBM per device.

v0:
```python
import jax
import jax.numpy as jnp
from jax import lax
from jax.sharding import PartitionSpec as P


def damped_inverse(summed, token_count, identity_matrix):
    proj_rank = identity_matrix.shape[0]
    covariance = summed / token_count
    damped = covariance + 0.1 * jnp.trace(covariance) / proj_rank * identity_matrix
    lower_factor = jnp.linalg.cholesky(damped)
    return jax.scipy.linalg.cho_solve((lower_factor, True), identity_matrix)


def precondition(query_rows, out_inverse, in_inverse):
    proj_rank = out_inverse.shape[0]
    query_mats = query_rows.astype(jnp.float32).reshape(query_rows.shape[0], proj_rank, proj_rank)
    half_done = jnp.einsum("ab,qbc->qac", out_inverse, query_mats, precision=lax.Precision.HIGHEST)
    precond = jnp.einsum("qac,cd->qad", half_done, in_inverse, precision=lax.Precision.HIGHEST)
    return precond.reshape(query_rows.shape[0], proj_rank * proj_rank).astype(jnp.bfloat16)


def project(tokens, projection):
    docs_here, length, features = tokens.shape
    flat = tokens.reshape(docs_here * length, features)
    result = lax.dot_general(
        flat, projection, (((1,), (1,)), ((), ())), preferred_element_type=jnp.float32
    )
    return result.reshape(docs_here, length, projection.shape[0])


def factor_totals(in_factor, out_factor, token_count):
    return lax.psum((in_factor, out_factor, token_count), ("grp", "fsdp"))


def shards(acts, out_grads, doc_lengths, proj_in, proj_out, store_grads, queries):
    docs_here, length, features = acts.shape
    proj_rank = proj_in.shape[0]
    identity_matrix = jnp.eye(proj_rank, dtype=jnp.float32)
    positions = lax.broadcasted_iota(jnp.int32, (docs_here, length), 1)
    valid_mask = (positions < doc_lengths[:, None]).astype(jnp.float32)
    in_proj = project(acts, proj_in)
    out_proj = project(out_grads, proj_out)
    in_masked = in_proj * valid_mask[:, :, None]
    out_masked = out_proj * valid_mask[:, :, None]
    in_factor = jnp.einsum("dta,dtb->ab", in_masked, in_proj, precision=lax.Precision.HIGHEST)
    out_factor = jnp.einsum("dta,dtb->ab", out_masked, out_proj, precision=lax.Precision.HIGHEST)
    token_count = jnp.sum(valid_mask)
    per_doc = jnp.einsum("dta,dtb->dab", out_masked, in_proj, precision=lax.Precision.HIGHEST)
    per_doc = per_doc / doc_lengths.astype(jnp.float32)[:, None, None]
    new_grads = per_doc.reshape(docs_here, proj_rank * proj_rank).astype(jnp.bfloat16)
    score_rows = jnp.concatenate([store_grads, new_grads], axis=0)
    stored = store_grads.shape[0]
    in_total, out_total, tokens_total = factor_totals(in_factor, out_factor, token_count)
    in_inverse = damped_inverse(in_total, tokens_total, identity_matrix)
    out_inverse = damped_inverse(out_total, tokens_total, identity_matrix)
    prepared_local = precondition(queries, out_inverse, in_inverse)
    scores = lax.dot_general(
        score_rows,
        lax.all_gather(prepared_local, "fsdp", axis=0, tiled=True),
        (((1,), (1,)), ((), ())),
        preferred_element_type=jnp.float32,
    )
    store_scores = scores[:stored].astype(jnp.bfloat16)
    new_scores = scores[stored:].astype(jnp.bfloat16)
    return (new_grads, store_scores, new_scores)


def solution(mesh):
    placed = (
        P(("grp", "fsdp"), None, None),
        P(("grp", "fsdp"), None, None),
        P(("grp", "fsdp")),
        P(),
        P(),
        P(("grp", "fsdp"), None),
        P("fsdp", None),
    )
    return jax.shard_map(
        shards,
        mesh=mesh,
        in_specs=placed,
        out_specs=(P(("grp", "fsdp"), None), P(("grp", "fsdp"), None), P(("grp", "fsdp"), None)),
        check_vma=False,
    )
```

profile of v0, /device:TPU:0, one launch (start us, length us, event | category | flops | bytes accessed | tf_op | source)
XLA Modules:
  0.0 139.9 jit_solution(4176288750345755124)
XLA Ops:
  7.2 0.0 copy-start
  7.2 0.0 copy-start.2
  7.2 0.0 copy-start.1
  7.2 0.0 all-gather.2.cloned.1.call-start
  7.2 1.5 %fusion.36 = f32[]{:T(128)} fusion(s32[2]{0:T(128)} %param.12), kind=kLoop, calls=%fused_computation.55 | loop fusion | flops 767 | bytes 12 | tf_op jit(solution)/shard_map/reduce_sum | solution.py:48
  8.7 0.7 compare_convert_fusion
  9.5 0.0 copy-done
  9.5 1.8 %fusion.13 = f32[2,128,64]{1,2,0:T(8,128)S(1)} fusion(bf16[2,128,4096]{2,1,0:T(8,128)(2,1)S(1)} %copy-done, bf16[64,4096]{1,0:T(8,128)(2,1)} %param.13), kind=kOutput, calls=%fused_computation.14 | convolution fusion | flops 134217728 | bytes 2686976 | tf_op jit(solution)/shard_map/dot_general | solution.py:26
  11.3 0.2 convolution_bitcast_fusion.1
  11.5 0.0 copy-done.2
  11.5 0.0 copy-done.1
  11.5 0.3 fusion.15
  11.8 0.2 convolution_bitcast_fusion.3
  12.0 42.9 %all-reduce = (f32[64,64]{0,1:T(8,128)S(1)}, f32[]{:T(128)}, f32[64,64]{0,1:T(8,128)S(1)}) all-reduce(f32[64,64]{0,1:T(8,128)S(1)} %convolution_bitcast_fusion.1, f32[]{:T(128)} %fusion.36, f32[64,64]{0,1:T(8,128)S(1)} %convolution_bitcast_fusion.3), channel_id=1, replica_groups=mesh['grp'=4,'fsdp'=8] {'grp','fsdp'}, use_global_device_ids=true, to_apply=%region_6.9 | all-reduce | flops 8193 | bytes 65544 | tf_op jit(solution)/shard_map/psum | solution.py:33
  54.9 1.3 select_reduce_fusion.3
  56.1 1.3 select_reduce_fusion.2
  58.7 0.7 select_add_fusion
  59.4 0.1 copy.13
  59.5 5.8 %cholesky.55 = f32[64,64]{1,0:T(8,128)S(1)} custom-call(f32[64,64]{1,0:T(8,128)S(1)} %fusion.28), custom_call_target="Cholesky" | custom-call | tf_op jit(solution)/shard_map/jit(cholesky)/cholesky | solution.py:11
  65.4 0.6 compare_reduce_fusion
  66.0 0.7 fusion.25
  66.7 4.9 %custom-call.9 = f32[1,64,64]{1,2,0:T(8,128)S(1)} custom-call(f32[1,64,64]{2,1,0:T(8,128)S(1)} %fusion.25), custom_call_target="InvertDiagBlocksLowerTriangular" | custom-call | tf_op jit(solution)/shard_map/jit(_cho_solve)/triangular_solve | solution.py:12
  71.6 0.3 fusion.20
  71.8 0.2 convolution_bitcast_fusion
  72.0 0.1 copy.11
  72.1 5.8 %cholesky.44 = f32[64,64]{1,0:T(8,128)S(1)} custom-call(f32[64,64]{1,0:T(8,128)S(1)} %fusion.31), custom_call_target="Cholesky" | custom-call | tf_op jit(solution)/shard_map/jit(cholesky)/cholesky | solution.py:11
  78.0 0.6 compare_reduce_fusion.1
  78.6 0.7 fusion.24
  79.3 4.9 %custom-call.8 = f32[1,64,64]{1,2,0:T(8,128)S(1)} custom-call(f32[1,64,64]{2,1,0:T(8,128)S(1)} %fusion.24), custom_call_target="InvertDiagBlocksLowerTriangular" | custom-call | tf_op jit(solution)/shard_map/jit(_cho_solve)/triangular_solve | solution.py:12
  84.2 0.3 fusion.22
  84.4 0.2 convolution_bitcast_fusion.2
  84.6 2.1 %reshape.52 = bf16[64,64,64]{2,1,0:T(8,128)(2,1)S(1)} reshape(bf16[64,4096]{1,0:T(8,128)(2,1)} %param.16) | data formatting | bytes 1048576 | tf_op jit(solution)/shard_map/reshape | solution.py:17
  86.7 1.0 fusion.37
  87.6 0.0 copy-start.4
  87.7 1.8 %fusion.6 = bf16[64,64,64]{2,1,0:T(8,128)(2,1)S(1)} fusion(f32[64,64,1]{1,0,2:T(8,128)S(1)} %convolution_bitcast_fusion, f32[64,64,64]{2,0,1:T(8,128)S(1)} %fusion.37), kind=kOutput, calls=%fused_computation.6 | convolution fusion | flops 201588736 | bytes 1589248 | tf_op jit(solution)/shard_map/qac,cd->qad/dot_general | solution.py:19
  89.4 1.6 %convert_element_type.36 = bf16[64,4096]{1,0:T(8,128)(2,1)} reshape(bf16[64,64,64]{2,1,0:T(8,128)(2,1)S(1)} %fusion.6) | data formatting | bytes 1048576 | tf_op jit(solution)/shard_map/convert_element_type | solution.py:20
  91.1 0.0 all-gather.2.cloned.1.call-update
  91.1 0.0 copy-done.4
  91.1 0.2 fusion.12
  91.3 0.1 convert_element_type.33
  91.4 0.0 copy-start.3
  91.5 36.3 %all-gather.2.cloned.1.call-done = bf16[512,4096]{1,0:T(8,128)(2,1)} async-done(((bf16[64,4096]{1,0:T(8,128)(2,1)}), bf16[512,4096]{1,0:T(8,128)(2,1)}) %all-gather.2.cloned.1.call-update) | async-done | bytes 4194320 | tf_op jit(solution)/shard_map/all_gather | solution.py:60
  127.8 4.0 %fusion.9 = bf16[226,512]{1,0:T(8,128)(2,1)S(1)} fusion(bf16[512,4096]{1,0:T(8,128)(2,1)} %all-gather.2.cloned.1.call-done, bf16[2,4096]{1,0:T(2,128)(2,1)S(1)} %convert_element_type.33, bf16[224,4096]{1,0:T(8,128)(2,1)} %param.15), kind=kOutput, calls=%fused_computation.7 | convolution fusion | flops 951731200 | bytes 6277120 | tf_op jit(solution)/shard_map/dot_general | solution.py:58
  131.8 0.0 copy-done.3
  131.8 0.6 slice.23
  132.4 0.7 slice.22
  (5 shorter events, 0.1 us)
Async XLA Ops:
  7.2 2.3 %copy-start = (bf16[2,128,4096]{2,1,0:T(8,128)(2,1)S(1)}, bf16[2,128,4096]{2,1,0:T(8,128)(2,1)}, u32[]{:S(2)}) copy-start(bf16[2,128,4096]{2,1,0:T(8,128)(2,1)} %param.10) | copy-start | bytes 6291460
  7.2 4.3 %copy-start.2 = (bf16[64,1024]{1,0:T(8,128)(2,1)S(1)}, bf16[64,1024]{1,0:T(8,128)(2,1)}, u32[]{:S(2)}) copy-start(bf16[64,1024]{1,0:T(8,128)(2,1)} %param.14) | copy-start | bytes 393220
  7.2 4.3 %copy-start.1 = (bf16[2,128,1024]{2,1,0:T(8,128)(2,1)S(1)}, bf16[2,128,1024]{2,1,0:T(8,128)(2,1)}, u32[]{:S(2)}) copy-start(bf16[2,128,1024]{2,1,0:T(8,128)(2,1)} %param.11) | copy-start | bytes 1572868
  7.2 120.6 %all-gather.2.cloned.1.call-start = ((), (), s32[]{:S(2)}) async-start(), calls=%async_computation | async-start | bytes 4718592 | tf_op jit(solution)/shard_map/all_gather | solution.py:60
  87.6 3.4 %copy-start.4 = (s32[2]{0:T(128)S(1)}, s32[2]{0:T(128)}, u32[]{:S(2)}) copy-start(s32[2]{0:T(128)} %param.12) | copy-start | bytes 28
  91.4 40.4 %copy-start.3 = (bf16[2,4096]{1,0:T(2,128)(2,1)}, bf16[2,4096]{1,0:T(2,128)(2,1)S(1)}, u32[]{:S(2)}) copy-start(bf16[2,4096]{1,0:T(2,128)(2,1)S(1)} %convert_element_type.33) | copy-start | bytes 49156
Sparse Core Ops, SparseCore 0:
  91.2 36.5 all-gather.1
where the time goes:
time: 140 us
  blocking collectives  42.9 us (31%)
  waiting for transfers between devices  36.3 us (26%)
  other arithmetic  29.5 us (21%)
  between operations  15.6 us (11%)
  matrix products  10.3 us (7%)
  local copies, waits for them, and re-layouts  5.25 us (4%)
    psum x1, blocking collectives, factor_totals(): return lax.psum((in_factor, out_factor, token_count), ('grp', 'fsdp'))  42.9 us
    all_gather x1, waiting for transfers between devices, shards(): lax.all_gather(prepared_local, 'fsdp', axis=0, tiled=True)  36.3 us
    another operation x6, other arithmetic, damped_inverse(): lower_factor = jnp.linalg.cholesky(damped)  13 us
    another operation x4, other arithmetic, damped_inverse(): return jax.scipy.linalg.cho_solve((lower_factor, True), identity_matrix)  11.1 us
    dot_general x1, matrix products, shards(): lax.dot_general(score_rows, lax.all_gather(prepared_local, 'fsdp', axis=0...  4.03 us
  transfers between devices with their start and end apart: 1, of which 1 were waited for; matrix products, arithmetic and copies ran while one was open for 0% of the time, Pallas kernels for 0%

commit v1 on v0

v1 whole, which is shorter than its diff:
```python
import functools

import jax
import jax.numpy as jnp
from jax import lax
from jax.experimental import pallas as pl
from jax.experimental.pallas import tpu as pltpu
from jax.sharding import PartitionSpec as P

F32 = jnp.float32
BF16 = jnp.bfloat16
ANY = pl.ANY
VMEM = pltpu.VMEM
HIGHEST = lax.Precision.HIGHEST
NT = (((1,), (1,)), ((), ()))
TN = (((0,), (0,)), ((), ()))


def invert_pair(matrix, rank):
    rows = lax.broadcasted_iota(jnp.int32, matrix.shape, 0)
    lanes = lax.broadcasted_iota(jnp.int32, matrix.shape, 1)
    left = lanes < rank
    local = jnp.where(left, lanes, lanes - rank)
    for k in range(rank):
        column = jnp.where(left, matrix[:, k : k + 1], matrix[:, rank + k : rank + k + 1])
        inverse_pivot = 1.0 / column[k : k + 1, :]
        at_pivot = local == k
        scaled = jnp.where(at_pivot[k : k + 1, :], 1.0, matrix[k : k + 1, :]) * inverse_pivot
        reduced = jnp.where(at_pivot, 0.0, matrix) - column * scaled
        matrix = jnp.where(rows == k, scaled, reduced)
    return matrix


def collect_kernel(
    n_grp, n_fsdp,
    lengths, acts, out_grads, proj_in, proj_out, queries,
    inverses, new_grads, gathered,
    acts_v, outg_v, pin_v, pout_v, plane_slots, column_slots, partial,
    load_sems, own_sem, gs, gr, fs, fr, ps, pr, cs, cr,
):
    g = lax.axis_index("grp")
    f = lax.axis_index("fsdp")
    n_docs, length, features = acts.shape
    rank = proj_in.shape[0]
    here = queries.shape[0]
    half = n_fsdp // 2
    partner = f + 1 - 2 * lax.rem(f, 2)

    loads = [
        pltpu.make_async_copy(src, dst, load_sems.at[i])
        for i, (src, dst) in enumerate(
            ((acts, acts_v), (proj_in, pin_v), (out_grads, outg_v), (proj_out, pout_v))
        )
    ]
    for load in loads:
        load.start()

    barrier = pltpu.get_barrier_semaphore()

    def greet_plane(d, _):
        pl.semaphore_signal(barrier, inc=1, device_id={"grp": g, "fsdp": lax.rem(f + d, n_fsdp)},
                            device_id_type=pl.DeviceIdType.MESH)
        return 0

    def greet_column(d, _):
        pl.semaphore_signal(barrier, inc=1, device_id={"grp": lax.rem(g + d, n_grp), "fsdp": f},
                            device_id_type=pl.DeviceIdType.MESH)
        return 0

    lax.fori_loop(1, n_fsdp, greet_plane, 0)
    lax.fori_loop(1, n_grp, greet_column, 0)
    pl.semaphore_wait(barrier, n_fsdp - 1 + n_grp - 1)

    def slot(index):
        return gathered.at[pl.ds(pl.multiple_of(index * here, here), here)]

    def shard_copy(d):
        return pltpu.make_async_remote_copy(
            src_ref=queries, dst_ref=slot(f), send_sem=gs.at[d], recv_sem=gr.at[d],
            device_id={"grp": g, "fsdp": lax.rem(f + 2 * d, n_fsdp)},
            device_id_type=pl.DeviceIdType.MESH)

    def pass_copy(d):
        source = lax.rem(f + n_fsdp - 2 * d, n_fsdp)
        return pltpu.make_async_remote_copy(
            src_ref=queries if d == 0 else slot(source), dst_ref=slot(f if d == 0 else source),
            send_sem=fs.at[d], recv_sem=fr.at[d],
            device_id={"grp": g, "fsdp": partner},
            device_id_type=pl.DeviceIdType.MESH)

    for d in range(1, half):
        shard_copy(d).start()
    pass_copy(0).start()
    own = pltpu.make_async_copy(queries, slot(f), own_sem)
    own.start()

    for load in loads:
        load.wait()
    tokens = lax.broadcasted_iota(jnp.int32, (length, 2 * rank), 0)
    lanes = lax.broadcasted_iota(jnp.int32, (rank, 2 * rank), 1)
    rows = lax.broadcasted_iota(jnp.int32, (rank, 2 * rank), 0)
    total = jnp.zeros((2 * rank, 2 * rank), F32)
    count = 0
    for doc in range(n_docs):
        in_proj = lax.dot_general(acts_v[doc], pin_v[...], NT, preferred_element_type=F32)
        out_proj = lax.dot_general(outg_v[doc], pout_v[...], NT, preferred_element_type=F32)
        both = jnp.concatenate([in_proj, out_proj], axis=1)
        size = lengths[doc]
        both = jnp.where(tokens < size, both, 0.0)
        gram = lax.dot_general(both, both, TN, precision=HIGHEST, preferred_element_type=F32)
        total = total + gram
        count = count + jnp.minimum(size, length)
        new_grads[doc] = (gram[rank:, :rank] / size.astype(F32)).astype(BF16)
    partial[0:rank, :] = jnp.where(lanes < rank, total[:rank, :], total[rank:, :])
    partial[rank:, :] = jnp.zeros((8, 2 * rank), F32) + count.astype(F32)

    def plane_copy(d):
        return pltpu.make_async_remote_copy(
            src_ref=partial, dst_ref=plane_slots.at[f], send_sem=ps.at[d], recv_sem=pr.at[d],
            device_id={"grp": g, "fsdp": lax.rem(f + d, n_fsdp)},
            device_id_type=pl.DeviceIdType.MESH)

    for d in range(1, n_fsdp):
        plane_copy(d).start()
    plane_slots[f] = partial[...]
    for d in range(1, n_fsdp):
        plane_copy(d).wait()
    summed = plane_slots[0]
    for i in range(1, n_fsdp):
        summed = summed + plane_slots[i]
    column_slots[g] = summed

    def column_copy(d):
        return pltpu.make_async_remote_copy(
            src_ref=column_slots.at[g], dst_ref=column_slots.at[g], send_sem=cs.at[d], recv_sem=cr.at[d],
            device_id={"grp": lax.rem(g + d, n_grp), "fsdp": f},
            device_id_type=pl.DeviceIdType.MESH)

    for d in range(1, n_grp):
        column_copy(d).start()
    for d in range(1, n_grp):
        column_copy(d).wait()
    summed = column_slots[0]
    for i in range(1, n_grp):
        summed = summed + column_slots[i]

    covariance = summed[:rank, :] / summed[rank : rank + 1, :]
    diagonal = (rows == lanes) | (rows + rank == lanes)
    on_diagonal = jnp.where(diagonal, covariance, 0.0)
    in_trace = jnp.sum(jnp.where(lanes < rank, on_diagonal, 0.0))
    out_trace = jnp.sum(jnp.where(lanes < rank, 0.0, on_diagonal))
    ridge = jnp.where(lanes < rank, 0.1 * in_trace / rank, 0.1 * out_trace / rank)
    inverses[...] = invert_pair(covariance + jnp.where(diagonal, ridge, 0.0), rank)

    own.wait()
    for d in range(1, half):
        shard_copy(d).wait()
        pass_copy(d).start()
    for d in range(half):
        pass_copy(d).wait()


def collect(n_grp, n_fsdp, doc_lengths, acts, out_grads, proj_in, proj_out, queries):
    n_docs, length, _ = acts.shape
    rank = proj_in.shape[0]
    here, width = queries.shape
    dma = pltpu.SemaphoreType.DMA
    return pl.pallas_call(
        functools.partial(collect_kernel, n_grp, n_fsdp),
        out_shape=(
            jax.ShapeDtypeStruct((rank, 2 * rank), F32),
            jax.ShapeDtypeStruct((n_docs, rank, rank), BF16),
            jax.ShapeDtypeStruct((n_fsdp * here, width), BF16),
        ),
        in_specs=[pl.BlockSpec(memory_space=pltpu.SMEM)] + [pl.BlockSpec(memory_space=ANY)] * 5,
        out_specs=(
            pl.BlockSpec(memory_space=VMEM),
            pl.BlockSpec(memory_space=VMEM),
            pl.BlockSpec(memory_space=ANY),
        ),
        scratch_shapes=[
            VMEM(acts.shape, BF16), VMEM(out_grads.shape, BF16),
            VMEM(proj_in.shape, BF16), VMEM(proj_out.shape, BF16),
            VMEM((n_fsdp, rank + 8, 2 * rank), F32), VMEM((n_grp, rank + 8, 2 * rank), F32),
            VMEM((rank + 8, 2 * rank), F32),
            dma((4,)), dma,
            dma((n_fsdp // 2,)), dma((n_fsdp // 2,)), dma((n_fsdp // 2,)), dma((n_fsdp // 2,)),
            dma((n_fsdp,)), dma((n_fsdp,)), dma((n_grp,)), dma((n_grp,)),
        ],
        compiler_params=pltpu.CompilerParams(
            collective_id=0, has_side_effects=True, vmem_limit_bytes=24 * 2**20),
    )(doc_lengths, acts, out_grads, proj_in, proj_out, queries)


def split3(value):
    high = value.astype(BF16)
    rest = value - high.astype(F32)
    middle = rest.astype(BF16)
    low = (rest - middle.astype(F32)).astype(BF16)
    return high, middle, low


def score_kernel(inverses, new_grads, queries, store, store_out, new_out, work, score_rows, sem):
    stored, width = store.shape
    fresh = new_grads.shape[0]
    rank = inverses.shape[0]
    rows_padded = score_rows.shape[0]
    load = pltpu.make_async_copy(store, score_rows.at[pl.ds(0, stored)], sem)
    load.start()
    pad = rows_padded - stored
    score_rows[stored:, :] = jnp.concatenate(
        [new_grads[...].astype(F32), jnp.zeros((pad - fresh, width), F32)], axis=0).astype(BF16)

    block = 4 * rank
    groups = work.shape[0]
    both = inverses[...]
    in_inverse = both[:, :rank]
    out_inverse = both[:, rank:]
    wide = jnp.concatenate([in_inverse] * 4, axis=1)
    tiled = jnp.concatenate([wide] * 4, axis=0)
    r = lax.broadcasted_iota(jnp.int32, (block, block), 0) // rank
    c = lax.broadcasted_iota(jnp.int32, (block, block), 1) // rank
    pieces = split3(jnp.where(r == c, tiled, 0.0))
    for i in range(width // block):
        chunk = queries[:, i * block : (i + 1) * block]
        part = lax.dot_general(pieces[0], chunk, NT, preferred_element_type=F32)
        part = part + lax.dot_general(pieces[1], chunk, NT, preferred_element_type=F32)
        part = part + lax.dot_general(pieces[2], chunk, NT, preferred_element_type=F32)
        for j in range(groups):
            work[j, i * block : (i + 1) * block, :] = part[:, j * 128 : (j + 1) * 128]

    oh, om, ol = split3(out_inverse)
    left = jnp.concatenate([oh, oh, om, om, oh, ol], axis=1)

    def one(b, _):
        where = pl.ds(b, rank, stride=rank)
        half_done = jnp.concatenate([work[j, where, :] for j in range(groups)], axis=1)
        xh, xm, xl = split3(half_done)
        right = jnp.concatenate([xh, xm, xh, xm, xl, xh], axis=0)
        done = jnp.dot(left, right, preferred_element_type=F32)
        for j in range(groups):
            work[j, where, :] = done[:, j * 128 : (j + 1) * 128]
        return 0

    lax.fori_loop(0, rank, one, 0, unroll=4)
    load.wait()
    prepared = jnp.concatenate([work[j].astype(BF16) for j in range(groups)], axis=1)
    scores = jnp.dot(score_rows[...], prepared, preferred_element_type=F32)
    store_out[...] = scores[:stored].astype(BF16)
    new_out[...] = scores[stored : stored + fresh].astype(BF16)


def score(inverses, new_grads, gathered, store_grads):
    stored, width = store_grads.shape
    fresh = new_grads.shape[0]
    n_queries = gathered.shape[0]
    rows_padded = (stored + fresh + 15) // 16 * 16
    return pl.pallas_call(
        score_kernel,
        out_shape=(
            jax.ShapeDtypeStruct((stored, n_queries), BF16),
            jax.ShapeDtypeStruct((fresh, n_queries), BF16),
        ),
        in_specs=[pl.BlockSpec(memory_space=VMEM)] * 3 + [pl.BlockSpec(memory_space=ANY)],
        out_specs=(pl.BlockSpec(memory_space=VMEM), pl.BlockSpec(memory_space=VMEM)),
        scratch_shapes=[
            VMEM((n_queries // 128, width, 128), F32), VMEM((rows_padded, width), BF16),
            pltpu.SemaphoreType.DMA,
        ],
        compiler_params=pltpu.CompilerParams(vmem_limit_bytes=48 * 2**20),
    )(inverses, new_grads, gathered, store_grads)


def solution(mesh):
    n_grp, n_fsdp = mesh.shape["grp"], mesh.shape["fsdp"]

    def shards(acts, out_grads, doc_lengths, proj_in, proj_out, store_grads, queries):
        inverses, per_doc, gathered = collect(
            n_grp, n_fsdp, doc_lengths, acts, out_grads, proj_in, proj_out, queries)
        new_grads = per_doc.reshape(per_doc.shape[0], -1)
        store_scores, new_scores = score(inverses, new_grads, gathered, store_grads)
        return new_grads, store_scores, new_scores

    rows = P(("grp", "fsdp"), None)
    placed = (
        P(("grp", "fsdp"), None, None),
        P(("grp", "fsdp"), None, None),
        P(("grp", "fsdp")),
        P(),
        P(),
        rows,
        P("fsdp", None),
    )
    return jax.shard_map(
        shards, mesh=mesh, in_specs=placed, out_specs=(rows, rows, rows), check_vma=False)
```

time: 140 us -> 83.2 us (0.59)
  Pallas kernels: 0 us -> 71.7 us
  blocking collectives: 42.9 us -> 0 us
  waiting for transfers between devices: 36.3 us -> 0 us
  other arithmetic: 29.5 us -> 0 us
  between operations: 15.6 us -> 0.68 us
  matrix products: 10.3 us -> 0 us
  local copies, waits for them, and re-layouts: 5.25 us -> 10.5 us
    pallas_call x0 -> x2, Pallas kernels: none -> 71.7 us  [the longest x1 47.3 us: collect(): pl.pallas_call(functools.partial(collect_kernel, n_grp, n_fsdp), out_shap...]
    psum x1 -> x0, blocking collectives: 42.9 us -> none  [factor_totals(): return lax.psum((in_factor, out_factor, token_count), ('grp', 'fsdp'))]
    all_gather x1 -> x0, waiting for transfers between devices: 36.3 us -> none  [shards(): lax.all_gather(prepared_local, 'fsdp', axis=0, tiled=True)]
    another operation x10 -> x0, other arithmetic: 24.1 us -> none  [the longest x6 13 us: damped_inverse(): lower_factor = jnp.linalg.cholesky(damped)]
    unnamed x10 -> x20, local copies, waits for them, and re-layouts: 0.03 us -> 10.4 us
    dot_general x8 -> x0, matrix products: 9.52 us -> none  [the longest x1 4.03 us: shards(): lax.dot_general(score_rows, lax.all_gather(prepared_local, 'fsdp', axis=0...]
    reduce_sum x3 -> x0, other arithmetic: 4 us -> none  [the longest x2 2.52 us: damped_inverse(): jnp.trace(covariance)]
    reshape x1, local copies, waits for them, and re-layouts: 2.06 us -> 0.1 us  [shards(): new_grads = per_doc.reshape(per_doc.shape[0], -1)]
  transfers between devices with their start and end apart: 1 -> 0, of which waited for: 1 -> 0; matrix products, arithmetic and copies ran while one was open for 0% -> 0% of each run, Pallas kernels for 0% -> 0%
where the time goes in v1:
time: 83.2 us; the launch traced here: 82.9 us
  Pallas kernels  71.7 us (86%)
  local copies, waits for them, and re-layouts  10.5 us (13%)
    pallas_call x1, Pallas kernels, collect(): pl.pallas_call(functools.partial(collect_kernel, n_grp, n_fsdp), out_shap...  47.3 us
    pallas_call x1, Pallas kernels, score(): pl.pallas_call(score_kernel, out_shape=(jax.ShapeDtypeStruct((stored, n_q...  24.4 us
    unnamed x20, local copies, waits for them, and re-layouts  10.4 us

profile of v1, /device:TPU:0, one launch (start us, length us, event | category | flops | bytes accessed | tf_op | source)
XLA Modules:
  0.0 82.9 jit_solution(6065426339062023828)
XLA Ops:
  0.6 0.0 copy-start.2
  0.6 1.6 %copy-done.2 = bf16[2,128,4096]{2,1,0:T(8,128)(2,1)S(1)} copy-done((bf16[2,128,4096]{2,1,0:T(8,128)(2,1)S(1)}, bf16[2,128,4096]{2,1,0:T(8,128)(2,1)}, u32[]{:S(2)}) %copy-start.2) | copy-done | bytes 2097176
  2.2 0.0 copy-start.4
  2.2 1.0 %copy-done.4 = bf16[2,128,1024]{2,1,0:T(8,128)(2,1)S(1)} copy-done((bf16[2,128,1024]{2,1,0:T(8,128)(2,1)S(1)}, bf16[2,128,1024]{2,1,0:T(8,128)(2,1)}, u32[]{:S(2)}) %copy-start.4) | copy-done | bytes 524312
  3.3 0.0 copy-start.5
  3.3 1.0 %copy-done.5 = bf16[64,4096]{1,0:T(8,128)(2,1)S(1)} copy-done((bf16[64,4096]{1,0:T(8,128)(2,1)S(1)}, bf16[64,4096]{1,0:T(8,128)(2,1)}, u32[]{:S(2)}) %copy-start.5) | copy-done | bytes 524312
  4.3 0.0 copy-start.6
  4.3 1.0 %copy-done.6 = bf16[64,4096]{1,0:T(8,128)(2,1)S(1)} copy-done((bf16[64,4096]{1,0:T(8,128)(2,1)S(1)}, bf16[64,4096]{1,0:T(8,128)(2,1)}, u32[]{:S(2)}) %copy-start.6) | copy-done | bytes 524312
  5.4 0.0 copy-start.7
  5.4 0.9 %copy-done.7 = bf16[64,1024]{1,0:T(8,128)(2,1)S(1)} copy-done((bf16[64,1024]{1,0:T(8,128)(2,1)S(1)}, bf16[64,1024]{1,0:T(8,128)(2,1)}, u32[]{:S(2)}) %copy-start.7) | copy-done | bytes 131096
  6.3 0.0 copy-start.9
  6.3 0.7 copy-done.9
  6.9 0.0 copy-start.3
  6.9 47.3 %shard_map.94 = (f32[64,128]{1,0:T(8,128)S(1)}, bf16[2,64,64]{2,1,0:T(8,128)(2,1)S(1)}, bf16[512,4096]{1,0:T(8,128)(2,1)S(1)}) custom-call(s32[2]{0:T(128)S(1)} %copy-done.9, bf16[2,128,4096]{2,1,0:T(8,128)(2,1)S(1)} %copy-done.2, bf16[2,128,1024]{2,1,0:T(8,128)(2,1)S(1)} %copy-done.4, bf16[64,4096]{1,0:T(8,128)(2,1)S(1)} %copy-done.5, ...), custom_call_target="tpu_custom_call" | custom-call | tf_op jit(solution)/shard_map/pallas_call | solution.py:168
  54.2 0.0 copy-start
  54.2 1.9 %copy-done = bf16[512,4096]{1,0:T(8,128)(2,1)} copy-done((bf16[512,4096]{1,0:T(8,128)(2,1)}, bf16[512,4096]{1,0:T(8,128)(2,1)S(1)}, u32[]{:S(2)}) %copy-start) | copy-done | bytes 4194328
  56.2 0.1 reshape.9.new_grads
  56.3 0.0 copy-done.3
  56.3 0.0 copy-start.1
  56.3 2.2 %copy-done.1 = bf16[512,4096]{1,0:T(8,128)(2,1)S(1)} copy-done((bf16[512,4096]{1,0:T(8,128)(2,1)S(1)}, bf16[512,4096]{1,0:T(8,128)(2,1)}, u32[]{:S(2)}) %copy-start.1) | copy-done | bytes 4194328
  58.5 0.0 copy-start.8
  58.5 24.4 %shard_map.95 = (bf16[224,512]{1,0:T(8,128)(2,1)}, bf16[2,512]{1,0:T(2,128)(2,1)}) custom-call(f32[64,128]{1,0:T(8,128)S(1)} %get-tuple-element.9.inverses, bf16[2,4096]{1,0:T(2,128)(2,1)S(1)} %reshape.9.new_grads, bf16[512,4096]{1,0:T(8,128)(2,1)S(1)} %copy-done.1, bf16[224,4096]{1,0:T(8,128)(2,1)S(1)} %copy-done.3), custom_call_target="tpu_custom_call" | custom-call | tf_op jit(solution)/shard_map/pallas_call | solution.py:258
  82.9 0.0 copy-done.8
Async XLA Ops:
  0.6 1.6 %copy-start.2 = (bf16[2,128,4096]{2,1,0:T(8,128)(2,1)S(1)}, bf16[2,128,4096]{2,1,0:T(8,128)(2,1)}, u32[]{:S(2)}) copy-start(bf16[2,128,4096]{2,1,0:T(8,128)(2,1)} %acts.1) | copy-start | bytes 6291460
  2.2 1.0 %copy-start.4 = (bf16[2,128,1024]{2,1,0:T(8,128)(2,1)S(1)}, bf16[2,128,1024]{2,1,0:T(8,128)(2,1)}, u32[]{:S(2)}) copy-start(bf16[2,128,1024]{2,1,0:T(8,128)(2,1)} %out_grads.1) | copy-start | bytes 1572868
  3.3 1.0 %copy-start.5 = (bf16[64,4096]{1,0:T(8,128)(2,1)S(1)}, bf16[64,4096]{1,0:T(8,128)(2,1)}, u32[]{:S(2)}) copy-start(bf16[64,4096]{1,0:T(8,128)(2,1)} %proj_in.1) | copy-start | bytes 1572868
  4.3 1.0 %copy-start.6 = (bf16[64,4096]{1,0:T(8,128)(2,1)S(1)}, bf16[64,4096]{1,0:T(8,128)(2,1)}, u32[]{:S(2)}) copy-start(bf16[64,4096]{1,0:T(8,128)(2,1)} %queries.1) | copy-start | bytes 1572868
  5.4 0.9 %copy-start.7 = (bf16[64,1024]{1,0:T(8,128)(2,1)S(1)}, bf16[64,1024]{1,0:T(8,128)(2,1)}, u32[]{:S(2)}) copy-start(bf16[64,1024]{1,0:T(8,128)(2,1)} %proj_out.1) | copy-start | bytes 393220
  6.3 0.7 copy-start.9
  6.9 49.4 %copy-start.3 = (bf16[224,4096]{1,0:T(8,128)(2,1)S(1)}, bf16[224,4096]{1,0:T(8,128)(2,1)}, u32[]{:S(2)}) copy-start(bf16[224,4096]{1,0:T(8,128)(2,1)} %store.1) | copy-start | bytes 5505028
  54.2 2.0 %copy-start = (bf16[512,4096]{1,0:T(8,128)(2,1)}, bf16[512,4096]{1,0:T(8,128)(2,1)S(1)}, u32[]{:S(2)}) copy-start(bf16[512,4096]{1,0:T(8,128)(2,1)S(1)} %get-tuple-element.10.queries) | copy-start | bytes 12582916
  56.3 2.2 %copy-start.1 = (bf16[512,4096]{1,0:T(8,128)(2,1)S(1)}, bf16[512,4096]{1,0:T(8,128)(2,1)}, u32[]{:S(2)}) copy-start(bf16[512,4096]{1,0:T(8,128)(2,1)} %copy-done) | copy-start | bytes 12582916
  58.5 24.4 %copy-start.8 = (bf16[2,4096]{1,0:T(2,128)(2,1)}, bf16[2,4096]{1,0:T(2,128)(2,1)S(1)}, u32[]{:S(2)}) copy-start(bf16[2,4096]{1,0:T(2,128)(2,1)S(1)} %reshape.9.new_grads) | copy-start | bytes 49156

commit v2 on v0

v2 whole, which is shorter than its diff:
```python
import functools

import jax
import jax.numpy as jnp
from jax import lax
from jax.experimental import pallas as pl
from jax.experimental.pallas import tpu as pltpu
from jax.sharding import PartitionSpec as P

F32 = jnp.float32
BF16 = jnp.bfloat16
ANY = pl.ANY
VMEM = pltpu.VMEM
HIGHEST = lax.Precision.HIGHEST
NT = (((1,), (1,)), ((), ()))
TN = (((0,), (0,)), ((), ()))


def invert_pair(matrix, rank):
    rows = lax.broadcasted_iota(jnp.int32, matrix.shape, 0)
    lanes = lax.broadcasted_iota(jnp.int32, matrix.shape, 1)
    left = lanes < rank
    local = jnp.where(left, lanes, lanes - rank)
    for k in range(rank):
        column = jnp.where(left, matrix[:, k : k + 1], matrix[:, rank + k : rank + k + 1])
        inverse_pivot = 1.0 / column[k : k + 1, :]
        at_pivot = local == k
        scaled = jnp.where(at_pivot[k : k + 1, :], 1.0, matrix[k : k + 1, :]) * inverse_pivot
        reduced = jnp.where(at_pivot, 0.0, matrix) - column * scaled
        matrix = jnp.where(rows == k, scaled, reduced)
    return matrix


def split3(value):
    high = value.astype(BF16)
    rest = value - high.astype(F32)
    middle = rest.astype(BF16)
    low = (rest - middle.astype(F32)).astype(BF16)
    return high, middle, low


def influence_kernel(
    n_grp, n_fsdp, early,
    lengths, acts, out_grads, proj_in, proj_out, queries, store,
    new_grads, store_out, new_out,
    acts_v, outg_v, pin_v, pout_v, gathered, score_rows, work, pieces, plane_slots, column_slots, totals,
    load_sems, gs, gr, fs, fr, ps, pr, cs, cr, ts, tr,
):
    g = lax.axis_index("grp")
    f = lax.axis_index("fsdp")
    n_docs, length, features = acts.shape
    rank = proj_in.shape[0]
    here, width = queries.shape
    stored = store.shape[0]
    half = n_fsdp // 2
    chip = f // 2
    core = lax.rem(f, 2)
    cut = here // PIECE
    share = rank // n_fsdp
    pitch = rank + 8
    mesh_id = pl.DeviceIdType.MESH

    def in_plane(d):
        return {"grp": g, "fsdp": lax.rem(f + d, n_fsdp)}

    def in_column(d):
        return {"grp": lax.rem(g + d, n_grp), "fsdp": f}

    def rows_of(index, p):
        return gathered.at[pl.ds(pl.multiple_of(index * here + p * PIECE, PIECE), PIECE)]

    def shard_copy(d, p):
        return pltpu.make_async_remote_copy(
            src_ref=queries.at[pl.ds(p * PIECE, PIECE)], dst_ref=rows_of(f, p),
            send_sem=gs.at[d * cut + p], recv_sem=gr.at[d * cut + p],
            device_id=in_plane(2 * d), device_id_type=mesh_id)

    def pass_copy(d, p):
        source = lax.rem(chip + half - d, half) * 2 + core
        return pltpu.make_async_remote_copy(
            src_ref=rows_of(source, p), dst_ref=rows_of(source, p),
            send_sem=fs.at[d * cut + p], recv_sem=fr.at[d * cut + p],
            device_id={"grp": g, "fsdp": f + 1 - 2 * core}, device_id_type=mesh_id)

    own_rows = gathered.at[pl.ds(pl.multiple_of(f * here, here), here)]
    loads = [
        pltpu.make_async_copy(src, dst, load_sems.at[i])
        for i, (src, dst) in enumerate((
            (acts, acts_v), (proj_in, pin_v), (out_grads, outg_v), (proj_out, pout_v),
            (queries, own_rows), (store, score_rows.at[pl.ds(0, stored)])))
    ]
    for load in loads:
        load.start()

    barrier = pltpu.get_barrier_semaphore()

    def greet_plane(d, _):
        pl.semaphore_signal(barrier, inc=1, device_id=in_plane(d), device_id_type=mesh_id)
        return 0

    def greet_column(d, _):
        pl.semaphore_signal(barrier, inc=1, device_id=in_column(d), device_id_type=mesh_id)
        return 0

    lax.fori_loop(1, n_fsdp, greet_plane, 0)
    lax.fori_loop(1, n_grp, greet_column, 0)
    pl.semaphore_wait(barrier, n_fsdp - 1 + n_grp - 1)

    for p in range(min(early, cut)):
        for d in range(1, half):
            shard_copy(d, p).start()
    for load in loads[:5]:
        load.wait()
    for p in range(cut):
        pass_copy(0, p).start()

    tokens = lax.broadcasted_iota(jnp.int32, (length, 2 * rank), 0)
    lanes = lax.broadcasted_iota(jnp.int32, (rank, 2 * rank), 1)
    rows = lax.broadcasted_iota(jnp.int32, (rank, 2 * rank), 0)
    total = jnp.zeros((2 * rank, 2 * rank), F32)
    count = 0
    per_doc = []
    for doc in range(n_docs):
        in_proj = lax.dot_general(acts_v[doc], pin_v[...], NT, preferred_element_type=F32)
        out_proj = lax.dot_general(outg_v[doc], pout_v[...], NT, preferred_element_type=F32)
        both = jnp.concatenate([in_proj, out_proj], axis=1)
        size = lengths[doc]
        both = jnp.where(tokens < size, both, 0.0)
        gram = lax.dot_general(both, both, TN, precision=HIGHEST, preferred_element_type=F32)
        total = total + gram
        count = count + jnp.minimum(size, length)
        per_doc.append(gram[rank:, :rank] / size.astype(F32))
    packed = jnp.where(lanes < rank, total[:rank, :], total[rank:, :])
    counts = jnp.zeros((8, 2 * rank), F32) + count.astype(F32)
    for i in range(n_fsdp):
        piece = packed[i * share : (i + 1) * share, :]
        if share < 8:
            piece = jnp.concatenate([piece, jnp.zeros((8 - share, 2 * rank), F32)], axis=0)
        pieces[i, : piece.shape[0], :] = piece
        pieces[i, piece.shape[0] :, :] = counts

    def scatter_copy(d):
        return pltpu.make_async_remote_copy(
            src_ref=pieces.at[lax.rem(f + d, n_fsdp)], dst_ref=plane_slots.at[f],
            send_sem=ps.at[d], recv_sem=pr.at[d], device_id=in_plane(d), device_id_type=mesh_id)

    def column_copy(d):
        return pltpu.make_async_remote_copy(
            src_ref=column_slots.at[g], dst_ref=column_slots.at[g],
            send_sem=cs.at[d], recv_sem=cr.at[d], device_id=in_column(d), device_id_type=mesh_id)

    def total_copy(d):
        return pltpu.make_async_remote_copy(
            src_ref=totals.at[f], dst_ref=totals.at[f],
            send_sem=ts.at[d], recv_sem=tr.at[d], device_id=in_plane(d), device_id_type=mesh_id)

    for d in range(1, n_fsdp):
        scatter_copy(d).start()
    plane_slots[f] = pieces[f]
    flat = [
        jnp.concatenate([grad[a : a + 1, :] for a in range(rank)], axis=1) for grad in per_doc
    ]
    fresh = jnp.concatenate(
        flat + [jnp.zeros((score_rows.shape[0] - stored - n_docs, width), F32)], axis=0).astype(BF16)
    score_rows[stored:, :] = fresh
    new_grads[...] = fresh[:n_docs]
    for d in range(1, n_fsdp):
        scatter_copy(d).wait()
    summed = plane_slots[0]
    for i in range(1, n_fsdp):
        summed = summed + plane_slots[i]
    column_slots[g] = summed
    for d in range(1, n_grp):
        column_copy(d).start()
    for d in range(1, n_grp):
        column_copy(d).wait()
    summed = column_slots[0]
    for i in range(1, n_grp):
        summed = summed + column_slots[i]
    totals[f] = summed
    for d in range(1, n_fsdp):
        total_copy(d).start()
    for p in range(min(early, cut), cut):
        for d in range(1, half):
            shard_copy(d, p).start()
    for d in range(1, n_fsdp):
        total_copy(d).wait()

    covariance = jnp.concatenate([totals[i, :share, :] for i in range(n_fsdp)], axis=0)
    covariance = covariance / summed[summed.shape[0] - 1 :, :]
    diagonal = (rows == lanes) | (rows + rank == lanes)
    on_diagonal = jnp.where(diagonal, covariance, 0.0)
    in_trace = jnp.sum(jnp.where(lanes < rank, on_diagonal, 0.0))
    out_trace = jnp.sum(jnp.where(lanes < rank, 0.0, on_diagonal))
    ridge = jnp.where(lanes < rank, 0.1 * in_trace / rank, 0.1 * out_trace / rank)
    both = invert_pair(covariance + jnp.where(diagonal, ridge, 0.0), rank)

    block = 4 * rank
    wide = jnp.concatenate([both[:, :rank]] * 4, axis=1)
    tiled = jnp.concatenate([wide] * 4, axis=0)
    r = lax.broadcasted_iota(jnp.int32, (block, block), 0) // rank
    c = lax.broadcasted_iota(jnp.int32, (block, block), 1) // rank
    in_parts = split3(jnp.where(r == c, tiled, 0.0))
    oh, om, ol = split3(both[:, rank:])
    left = jnp.concatenate([oh, oh, om, om, oh, ol], axis=1)

    load = loads[5]
    load.wait()
    unit_chips = UNIT // (2 * here)
    n_units = half // unit_chips

    def one_unit(e, _):
        unit = lax.rem(chip // unit_chips + n_units - e, n_units)
        for i in range(unit_chips):
            d = lax.rem(chip - (unit * unit_chips + i) + half, half)

            @pl.when(d != 0)
            def _():
                for p in range(cut):
                    shard_copy(d, p).wait()
                    pass_copy(d, p).start()

        for i in range(unit_chips):
            d = lax.rem(chip - (unit * unit_chips + i) + half, half)
            for p in range(cut):
                pass_copy(d, p).wait()
        here_rows = pl.ds(pl.multiple_of(unit * UNIT, UNIT), UNIT)
        for i in range(width // block):
            chunk = gathered[here_rows, i * block : (i + 1) * block]
            part = lax.dot_general(in_parts[0], chunk, NT, preferred_element_type=F32)
            part = part + lax.dot_general(in_parts[1], chunk, NT, preferred_element_type=F32)
            part = part + lax.dot_general(in_parts[2], chunk, NT, preferred_element_type=F32)
            for a in range(4):
                start = (4 * i + a) * pitch
                work[start : start + rank, :] = part[a * rank : (a + 1) * rank, :]
        for b in range(0, rank, 4):
            wheres = [pl.ds(b + j, rank, stride=pitch) for j in range(4)]
            half_done = jnp.concatenate([work[w, :] for w in wheres], axis=1)
            xh, xm, xl = split3(half_done)
            right = jnp.concatenate([xh, xm, xh, xm, xl, xh], axis=0)
            done = jnp.dot(left, right, preferred_element_type=F32)
            for j in range(4):
                work[wheres[j], :] = done[:, j * UNIT : (j + 1) * UNIT]
        prepared = jnp.concatenate(
            [work[a * pitch : a * pitch + rank, :].astype(BF16) for a in range(rank)], axis=0)
        scores = jnp.dot(score_rows[...], prepared, preferred_element_type=F32).astype(BF16)
        store_out[:, here_rows] = scores[:stored]
        new_out[:, here_rows] = scores[stored : stored + n_docs]
        return 0

    lax.fori_loop(0, n_units, one_unit, 0)


PIECE = 16
UNIT = 128


def influence(n_grp, n_fsdp, early, doc_lengths, acts, out_grads, proj_in, proj_out, queries, store):
    n_docs = acts.shape[0]
    rank = proj_in.shape[0]
    here, width = queries.shape
    stored = store.shape[0]
    n_queries = n_fsdp * here
    dma = pltpu.SemaphoreType.DMA
    slot = (-(-(rank // n_fsdp) // 8) * 8 + 8, 2 * rank)
    score_rows = -(-(stored + n_docs) // 16) * 16
    copies = dma((n_fsdp // 2 * (here // PIECE),))
    return pl.pallas_call(
        functools.partial(influence_kernel, n_grp, n_fsdp, early),
        out_shape=(
            jax.ShapeDtypeStruct((n_docs, width), BF16),
            jax.ShapeDtypeStruct((stored, n_queries), BF16),
            jax.ShapeDtypeStruct((n_docs, n_queries), BF16),
        ),
        in_specs=[pl.BlockSpec(memory_space=pltpu.SMEM)] + [pl.BlockSpec(memory_space=ANY)] * 6,
        out_specs=tuple([pl.BlockSpec(memory_space=VMEM)] * 3),
        scratch_shapes=[
            VMEM(acts.shape, BF16), VMEM(out_grads.shape, BF16),
            VMEM(proj_in.shape, BF16), VMEM(proj_out.shape, BF16),
            VMEM((n_queries, width), BF16), VMEM((score_rows, width), BF16),
            VMEM((rank * (rank + 8), UNIT), F32),
            VMEM((n_fsdp,) + slot, F32), VMEM((n_fsdp,) + slot, F32),
            VMEM((n_grp,) + slot, F32), VMEM((n_fsdp,) + slot, F32),
            dma((6,)), copies, copies, copies, copies,
            dma((n_fsdp,)), dma((n_fsdp,)), dma((n_grp,)), dma((n_grp,)), dma((n_fsdp,)), dma((n_fsdp,)),
        ],
        compiler_params=pltpu.CompilerParams(
            collective_id=0, has_side_effects=True, vmem_limit_bytes=60 * 2**20),
    )(doc_lengths, acts, out_grads, proj_in, proj_out, queries, store)


def solution(mesh):
    n_grp, n_fsdp = mesh.shape["grp"], mesh.shape["fsdp"]

    def shards(acts, out_grads, doc_lengths, proj_in, proj_out, store_grads, queries):
        return influence(
            n_grp, n_fsdp, 1, doc_lengths, acts, out_grads, proj_in, proj_out, queries, store_grads)

    rows = P(("grp", "fsdp"), None)
    placed = (
        P(("grp", "fsdp"), None, None),
        P(("grp", "fsdp"), None, None),
        P(("grp", "fsdp")),
        P(),
        P(),
        rows,
        P("fsdp", None),
    )
    return jax.shard_map(
        shards, mesh=mesh, in_specs=placed, out_specs=(rows, rows, rows), check_vma=False)
```

time: 140 us -> 58.7 us (0.42)
  Pallas kernels: 0 us -> 53.5 us
  blocking collectives: 42.9 us -> 0 us
  waiting for transfers between devices: 36.3 us -> 0 us
  other arithmetic: 29.5 us -> 0 us
  between operations: 15.6 us -> 0.64 us
  matrix products: 10.3 us -> 0 us
    pallas_call x0 -> x1, Pallas kernels: none -> 53.5 us  [influence(): pl.pallas_call(functools.partial(influence_kernel, n_grp, n_fsdp, early),...]
    psum x1 -> x0, blocking collectives: 42.9 us -> none  [factor_totals(): return lax.psum((in_factor, out_factor, token_count), ('grp', 'fsdp'))]
    all_gather x1 -> x0, waiting for transfers between devices: 36.3 us -> none  [shards(): lax.all_gather(prepared_local, 'fsdp', axis=0, tiled=True)]
    another operation x10 -> x0, other arithmetic: 24.1 us -> none  [the longest x6 13 us: damped_inverse(): lower_factor = jnp.linalg.cholesky(damped)]
    dot_general x8 -> x0, matrix products: 9.52 us -> none  [the longest x1 4.03 us: shards(): lax.dot_general(score_rows, lax.all_gather(prepared_local, 'fsdp', axis=0...]
    unnamed x10 -> x3, local copies, waits for them, and re-layouts: 0.03 us -> 4.22 us
    reduce_sum x3 -> x0, other arithmetic: 4 us -> none  [the longest x2 2.52 us: damped_inverse(): jnp.trace(covariance)]
    reshape x1 -> x0, local copies, waits for them, and re-layouts: 2.06 us -> none  [precondition(): query_rows.astype(jnp.float32)]
  transfers between devices with their start and end apart: 1 -> 0, of which waited for: 1 -> 0; matrix products, arithmetic and copies ran while one was open for 0% -> 0% of each run, Pallas kernels for 0% -> 0%
where the time goes in v2:
time: 58.7 us; the launch traced here: 58.4 us
  Pallas kernels  53.5 us (91%)
  local copies, waits for them, and re-layouts  4.22 us (7%)
  between operations  0.64 us (1%)
    pallas_call x1, Pallas kernels, influence(): pl.pallas_call(functools.partial(influence_kernel, n_grp, n_fsdp, early),...  53.5 us
    unnamed x3, local copies, waits for them, and re-layouts  4.22 us

profile of v2, /device:TPU:0, one launch (start us, length us, event | category | flops | bytes accessed | tf_op | source)
XLA Modules:
  0.0 58.4 jit_solution(15066398440464581700)
XLA Ops:
  0.6 53.5 %shard_map.94 = (bf16[2,4096]{1,0:T(2,128)(2,1)}, bf16[224,512]{1,0:T(8,128)(2,1)}, bf16[2,512]{1,0:T(2,128)(2,1)}) custom-call(s32[2]{0:T(128)} %lengths.1, bf16[2,128,4096]{2,1,0:T(8,128)(2,1)} %acts.1, bf16[2,128,1024]{2,1,0:T(8,128)(2,1)} %out_grads.1, bf16[64,4096]{1,0:T(8,128)(2,1)} %proj_in.1, bf16[64,1024]{1,0:T(8,128)(2,1)} %proj_out.1, ...), custom_call_target="tpu_custom_call" | custom-call | tf_op jit(solution)/shard_map/pallas_call | solution.py:268
  54.2 1.3 %copy.13 = bf16[2,4096]{1,0:T(2,128)(2,1)} copy(bf16[2,4096]{1,0:T(2,128)(2,1)} %get-tuple-element.6) | data formatting | bytes 32768
  55.5 1.6 %copy.14 = bf16[224,512]{1,0:T(8,128)(2,1)} copy(bf16[224,512]{1,0:T(8,128)(2,1)} %get-tuple-element.7) | data formatting | bytes 458752
  57.1 1.2 %copy.15 = bf16[2,512]{1,0:T(2,128)(2,1)} copy(bf16[2,512]{1,0:T(2,128)(2,1)} %get-tuple-element.8) | data formatting | bytes 4096

commit v3 on v2

--- a/solution.py
+++ b/solution.py
@@ -172,6 +172,9 @@
     column_slots[g] = summed
     for d in range(1, n_grp):
         column_copy(d).start()
+    for p in range(min(early, cut), min(2 * early, cut)):
+        for d in range(1, half):
+            shard_copy(d, p).start()
     for d in range(1, n_grp):
         column_copy(d).wait()
     summed = column_slots[0]
@@ -180,8 +183,8 @@
     totals[f] = summed
     for d in range(1, n_fsdp):
         total_copy(d).start()
-    for p in range(min(early, cut), cut):
-        for d in range(1, half):
+    for d in range(1, half):
+        for p in range(min(2 * early, cut), cut):
             shard_copy(d, p).start()
     for d in range(1, n_fsdp):
         total_copy(d).wait()

time: 58.7 us -> 56.3 us (0.959)
  Pallas kernels: 53.5 us -> 51.2 us
    pallas_call x1, Pallas kernels: 53.5 us -> 51.2 us  [influence(): pl.pallas_call(functools.partial(influence_kernel, n_grp, n_fsdp, early),...]
where the time goes in v3:
time: 56.3 us; the launch traced here: 56 us
  Pallas kernels  51.2 us (91%)
  local copies, waits for them, and re-layouts  4.22 us (7%)
  between operations  0.64 us (1%)
    pallas_call x1, Pallas kernels, influence(): pl.pallas_call(functools.partial(influence_kernel, n_grp, n_fsdp, early),...  51.2 us
    unnamed x3, local copies, waits for them, and re-layouts  4.22 us

profile of v3, /device:TPU:0, one launch (start us, length us, event | category | flops | bytes accessed | tf_op | source)
XLA Modules:
  0.0 56.0 jit_solution(14964024891898534404)
XLA Ops:
  0.6 51.2 %shard_map.94 = (bf16[2,4096]{1,0:T(2,128)(2,1)}, bf16[224,512]{1,0:T(8,128)(2,1)}, bf16[2,512]{1,0:T(2,128)(2,1)}) custom-call(s32[2]{0:T(128)} %lengths.1, bf16[2,128,4096]{2,1,0:T(8,128)(2,1)} %acts.1, bf16[2,128,1024]{2,1,0:T(8,128)(2,1)} %out_grads.1, bf16[64,4096]{1,0:T(8,128)(2,1)} %proj_in.1, bf16[64,1024]{1,0:T(8,128)(2,1)} %proj_out.1, ...), custom_call_target="tpu_custom_call" | custom-call | tf_op jit(solution)/shard_map/pallas_call | solution.py:271
  51.8 1.3 %copy.13 = bf16[2,4096]{1,0:T(2,128)(2,1)} copy(bf16[2,4096]{1,0:T(2,128)(2,1)} %get-tuple-element.6) | data formatting | bytes 32768
  53.1 1.6 %copy.14 = bf16[224,512]{1,0:T(8,128)(2,1)} copy(bf16[224,512]{1,0:T(8,128)(2,1)} %get-tuple-element.7) | data formatting | bytes 458752
  54.8 1.2 %copy.15 = bf16[2,512]{1,0:T(2,128)(2,1)} copy(bf16[2,512]{1,0:T(2,128)(2,1)} %get-tuple-element.8) | data formatting | bytes 4096
